TPU v7x, 256 devices: a whole 4x4x8 slice. The times are simulated.
256 devices in a mesh: blk: 32 (over y, z_hi, core), ij: 8 (over z_lo, x).
Axes of the slice: x: 4, y: 4, z: 8 (z_hi: 4, z_lo: 2; z = z_hi * 2 + z_lo), core: 2. Of those that a mesh axis runs over, the one named last changes fastest.
Arguments:
- density: float32 [32, 6, 256, 128], P('blk', None, 'ij'), may hold values from 0.8 to 1.2
- momentum: float32 [32, 3, 6, 256, 128], P('blk', None, None, 'ij'), may hold values from -2.5 to 2.5
- energy: float32 [32, 6, 256, 128], P('blk', None, 'ij'), may hold values from 2.5 to 4
- metrics: float32 [32, 4, 256, 128], P('blk', None, 'ij'), may hold values from -1 to 1
- volume: float32 [32, 256, 128], P('blk', 'ij'), may hold values from 0.5 to 2
- placed: int32 [32], replicated, may hold values from 0 to 31, each once
- neighbour: int32 [32, 2], replicated, may hold values from 0 to 31, as said below
- face: int32 [32, 2], replicated, may hold values from 0 to 1, as said below
- orient: int32 [32, 2], replicated, may hold values from 0 to 1, as said below
Outputs:
- next_density: float32 [32, 6, 256, 128], P('blk', None, 'ij')
- next_momentum: float32 [32, 3, 6, 256, 128], P('blk', None, None, 'ij')
- next_energy: float32 [32, 6, 256, 128], P('blk', None, 'ij')
Inputs may be any that keep to these rules, and one draw needn't show every extreme that they name: If face f of block b meets face g of block c with orientation o, then face g of c meets face f of b with orientation o; every block id appears as a neighbour. `face`: consistent with neighbour as stated there. `orient`: consistent with neighbour as stated there.
All inputs are finite; a program needn't handle non-finite values.
Results may differ from a plain program's by a relative error of at most 0.00002.
Values sent between devices are 32-bit elements; how exact they have to be, the bound alone decides.
A program may use at most 128 MiB of HBM per device.

v0:
```python
import jax
import jax.numpy as jnp
from jax import lax
from jax.sharding import PartitionSpec as P

pressure_factor = 0.4
viscosity = 0.05
conduction = 0.1
time_step = 0.03


def extended(value, sides, width):
    for axis, dim in sides:
        size, length = (lax.axis_size(axis), value.shape[dim])
        up = [(i, (i + 1) % size) for i in range(size - 1)]
        down = [(j, i) for i, j in up]
        last = lax.slice_in_dim(value, length - width, length, axis=dim)
        initial = lax.slice_in_dim(value, 0, width, axis=dim)
        before = lax.ppermute(last, axis, up)
        after = lax.ppermute(initial, axis, down)
        value = jnp.concatenate([before, value, after], axis=dim)
    return value


def slope_rows(f):
    return (
        f[..., 0:-4, 2:-2] - 8.0 * f[..., 1:-3, 2:-2] + 8.0 * f[..., 3:-1, 2:-2] - f[..., 4:, 2:-2]
    ) / 12.0


def slope_cols(f):
    return (
        f[..., 2:-2, 0:-4] - 8.0 * f[..., 2:-2, 1:-3] + 8.0 * f[..., 2:-2, 3:-1] - f[..., 2:-2, 4:]
    ) / 12.0


def slope_planes(f):
    return (
        jnp.roll(f, 2, -3)
        - 8.0 * jnp.roll(f, 1, -3)
        + 8.0 * jnp.roll(f, -1, -3)
        - jnp.roll(f, -2, -3)
    ) / 12.0


def curve_rows(f):
    return (
        -f[..., 0:-4, 2:-2]
        + 16.0 * f[..., 1:-3, 2:-2]
        - 30.0 * f[..., 2:-2, 2:-2]
        + 16.0 * f[..., 3:-1, 2:-2]
        - f[..., 4:, 2:-2]
    ) / 12.0


def curve_cols(f):
    return (
        -f[..., 2:-2, 0:-4]
        + 16.0 * f[..., 2:-2, 1:-3]
        - 30.0 * f[..., 2:-2, 2:-2]
        + 16.0 * f[..., 2:-2, 3:-1]
        - f[..., 2:-2, 4:]
    ) / 12.0


def curve_planes(f):
    return (
        -jnp.roll(f, 2, -3)
        + 16.0 * jnp.roll(f, 1, -3)
        - 30.0 * f
        + 16.0 * jnp.roll(f, -1, -3)
        - jnp.roll(f, -2, -3)
    ) / 12.0


def interior(f):
    return f[..., 2:-2, 2:-2]


def residual(ext):
    planes = ext.shape[1] - 1
    fields = ext[:, :planes]
    metric = ext[:, planes]
    dens = fields[0]
    moment = fields[1:4]
    energy_now = fields[4]
    velocity = moment / dens
    kinetic = 0.5 * jnp.sum(moment * velocity, axis=0)
    pressure = pressure_factor * (energy_now - kinetic)
    thermal = pressure / dens
    total_head = energy_now + pressure
    row_ax, row_ay, col_bx, col_by, cell_vol = (
        metric[0],
        metric[1],
        metric[2],
        metric[3],
        metric[4],
    )
    along_rows = row_ax * velocity[0] + row_ay * velocity[1]
    along_cols = col_bx * velocity[0] + col_by * velocity[1]
    flux_rows = cell_vol * jnp.stack(
        [
            dens * along_rows,
            moment[0] * along_rows + row_ax * pressure,
            moment[1] * along_rows + row_ay * pressure,
            moment[2] * along_rows,
            total_head * along_rows,
        ]
    )
    flux_cols = cell_vol * jnp.stack(
        [
            dens * along_cols,
            moment[0] * along_cols + col_bx * pressure,
            moment[1] * along_cols + col_by * pressure,
            moment[2] * along_cols,
            total_head * along_cols,
        ]
    )
    flux_planes = jnp.stack(
        [
            moment[2],
            moment[0] * velocity[2],
            moment[1] * velocity[2],
            moment[2] * velocity[2] + pressure,
            total_head * velocity[2],
        ]
    )
    inviscid = -(slope_rows(flux_rows) + slope_cols(flux_cols)) / interior(cell_vol) - slope_planes(
        interior(flux_planes)
    )
    row_weight = interior(row_ax * row_ax + row_ay * row_ay)
    col_weight = interior(col_bx * col_bx + col_by * col_by)

    def laplace(w):
        return row_weight * curve_rows(w) + col_weight * curve_cols(w) + curve_planes(interior(w))

    half_speed = kinetic / dens
    diffuse = jnp.stack(
        [
            jnp.zeros_like(inviscid[0]),
            viscosity * laplace(velocity[0]),
            viscosity * laplace(velocity[1]),
            viscosity * laplace(velocity[2]),
            viscosity * laplace(half_speed) + conduction * laplace(thermal),
        ]
    )
    return inviscid + diffuse


def wall_signs(planes):
    channel = jnp.arange(5)[:, None]
    plane_index = jnp.arange(planes)[None, :]
    flipped = (channel >= 1) & (channel <= 3) & (plane_index < planes - 1)
    return jnp.where(flipped, -1.0, 1.0)[:, :, None, None]


def ghost_factors(twisted, facing, planes):
    own_face = jnp.arange(2)[None, :]
    turn = jnp.where(twisted == 1, -1.0, 1.0)
    same = jnp.where(facing == own_face, -1.0, 1.0)
    channel = jnp.arange(5)[None, None, :]
    by_channel = jnp.where(
        channel < 2, turn[:, :, None], jnp.where(channel < 4, same[:, :, None], 1.0)
    )
    metric_plane = (jnp.arange(planes) == planes - 1)[None, None, None, :]
    return jnp.where(metric_plane, by_channel[:, :, :, None], 1.0)


def locate(placed):
    blocks = placed.shape[0]
    slots = jnp.arange(blocks, dtype=jnp.int32)
    return jnp.sum(jnp.where(placed[:, None] == slots[None, :], slots[:, None], 0), axis=0)


def pick_faces(target, facing, piece):
    piece_rows = piece.shape[0]
    slot_index = jnp.arange(piece_rows, dtype=jnp.int32)
    matched = target[:, :, None] == slot_index[None, None, :]
    chosen = jnp.where(
        facing[:, :, None, None, None, None, None] == 1,
        piece[None, None, :, 1],
        piece[None, None, :, 0],
    )
    return jnp.sum(jnp.where(matched[:, :, :, None, None, None, None], chosen, 0.0), axis=2)


def local(density, momentum, energy, metrics, volume, placed, neighbour, face, orient):
    local_count = density.shape[0]
    planes = density.shape[1] + 1
    fields = jnp.concatenate([density[:, None], momentum, energy[:, None]], axis=1)
    metric_plane = jnp.concatenate([metrics, volume[:, None]], axis=1)[:, :, None]
    split_count = lax.axis_size("ij")
    split_index = lax.axis_index("ij")
    group_index = lax.axis_index("blk")
    position = group_index * local_count + jnp.arange(local_count, dtype=jnp.int32)
    own_ids = placed[position]
    position_of = locate(placed)
    next_ids = neighbour[own_ids]
    facing = face[own_ids]
    twisted = orient[own_ids]
    partner = position_of[next_ids]
    factor = ghost_factors(twisted, facing, planes)[:, :, None, :, :, None]
    signs = wall_signs(planes)

    def extend(base):
        padded = extended(base, (("ij", 3),), 2)
        low_wall = base[:, :, :, 1::-1] * signs
        high_wall = base[:, :, :, -1:-3:-1]
        low_rows = jnp.where(split_index == 0, low_wall, padded[:, :, :, 0:2])
        high_rows = jnp.where(split_index == split_count - 1, high_wall, padded[:, :, :, -2:])
        rowed = jnp.concatenate([low_rows, base, high_rows], axis=3)
        strips = jnp.moveaxis(jnp.stack([base[..., 0:2], base[..., -1:-3:-1]], axis=1), -1, 2)
        source = partner // local_count * split_count + jnp.where(
            twisted == 1, split_count - 1 - split_index, split_index
        )
        target = source * local_count + partner % local_count
        ghosts = pick_faces(
            target, facing, lax.all_gather(strips, ("blk", "ij"), axis=0, tiled=True)
        )
        ghosts = jnp.where(twisted[:, :, None, None, None, None] == 1, ghosts[..., ::-1], ghosts)
        ghosts = jnp.moveaxis(ghosts * factor, 2, -1)
        left = jnp.pad(
            ghosts[:, 0][..., ::-1], ((0, 0), (0, 0), (0, 0), (2, 2), (0, 0)), constant_values=1.0
        )
        right = jnp.pad(ghosts[:, 1], ((0, 0), (0, 0), (0, 0), (2, 2), (0, 0)), constant_values=1.0)
        return jnp.concatenate([left, rowed, right], axis=-1)

    def tendency(state):
        return jax.vmap(residual)(extend(jnp.concatenate([state, metric_plane], axis=2)))

    section = fields + time_step * tendency(fields)
    result = 0.5 * fields + 0.5 * (section + time_step * tendency(section))
    return (result[:, 0], result[:, 1:4], result[:, 4])


def solution(mesh):
    return jax.shard_map(
        local,
        mesh=mesh,
        in_specs=(
            P("blk", None, "ij", None),
            P("blk", None, None, "ij", None),
            P("blk", None, "ij", None),
            P("blk", None, "ij", None),
            P("blk", "ij", None),
            P(),
            P(),
            P(),
            P(),
        ),
        out_specs=(
            P("blk", None, "ij", None),
            P("blk", None, None, "ij", None),
            P("blk", None, "ij", None),
        ),
        check_vma=False,
    )
```

profile of v0, /device:TPU:99, one launch (start us, length us, event | category | flops | bytes accessed | tf_op | source)
XLA Modules:
  0.0 1607.6 jit_solution(9384204103739592441)
XLA Ops:
  7.2 0.9 fusion.228
  8.1 1.1 fusion.49
  11.5 3.1 collective-permute-start
  14.6 2.2 collective-permute-start.1
  22.1 733.1 %all-gather.3.cloned.1.call-done = f32[256,2,2,5,7,32]{5,2,4,3,1,0:T(2,128)} async-done(((f32[1,2,2,5,7,32]{5,2,4,3,1,0:T(2,128)}), f32[256,2,2,5,7,32]{5,2,4,3,1,0:T(2,128)}) %all-gather.3.cloned.1.call-update) | async-done | bytes 4587536 | tf_op jit(solution)/shard_map/all_gather | solution.py:218
  755.1 18.2 %slice_bitcast_fusion.3 = (f32[256,2,5,7,32]{4,1,3,2,0:T(2,128)}, f32[256,2,5,7,32]{4,1,3,2,0:T(2,128)}) fusion(f32[256,2,2,5,7,32]{5,2,4,3,1,0:T(2,128)} %all-gather.3.cloned.1.call-done), kind=kLoop, calls=%fused_computation.4 | loop fusion | bytes 9175040 | tf_op jit(solution)/shard_map/jit(_where)/broadcast_in_dim | solution.py:179
  773.4 9.6 copy.248
  782.9 11.1 copy.249
  794.1 2.6 select_reduce_fusion.1
  803.3 0.9 fusion.170
  804.2 0.9 fusion.157
  805.1 0.9 fusion.144
  806.0 1.1 fusion.120
  807.2 2.1 multiply_add_fusion
  812.2 1.9 collective-permute-start.3
  814.1 3.5 collective-permute-start.2
  817.9 0.9 collective-permute-done.2
  818.9 729.0 %all-gather.5.cloned.1.call-done = f32[256,2,2,5,7,32]{5,2,4,3,1,0:T(2,128)} async-done(((f32[1,2,2,5,7,32]{5,2,4,3,1,0:T(2,128)}), f32[256,2,2,5,7,32]{5,2,4,3,1,0:T(2,128)}) %all-gather.5.cloned.1.call-update) | async-done | bytes 4587536 | tf_op jit(solution)/shard_map/all_gather | solution.py:218
  1548.0 18.2 %slice_bitcast_fusion.1 = (f32[256,2,5,7,32]{4,1,3,2,0:T(2,128)}, f32[256,2,5,7,32]{4,1,3,2,0:T(2,128)}) fusion(f32[256,2,2,5,7,32]{5,2,4,3,1,0:T(2,128)} %all-gather.5.cloned.1.call-done), kind=kLoop, calls=%fused_computation.2 | loop fusion | bytes 9175040 | tf_op jit(solution)/shard_map/jit(_where)/broadcast_in_dim | solution.py:179
  1566.2 9.6 copy.281
  1575.8 11.1 copy.282
  1586.9 2.6 select_reduce_fusion
  1596.1 0.9 copy-done.5
  1598.3 1.0 add_multiply_fusion
  (183 shorter events, 24.2 us)
Async XLA Ops:
  7.2 12.2 copy-start
  7.2 747.9 %all-gather.3.cloned.1.call-start = ((), (), s32[]{:S(2)}) async-start(), calls=%async_computation | async-start | bytes 18421760 | tf_op jit(solution)/shard_map/all_gather | solution.py:218
  10.4 6.5 copy-start.8
  10.4 9.2 copy-start.6
  10.6 9.8 copy-start.7
  11.4 1536.6 %all-gather.5.cloned.1.call-start = ((), (), s32[]{:S(2)}) async-start(), calls=%async_computation.1 | async-start | bytes 18421760 | tf_op jit(solution)/shard_map/all_gather | solution.py:218
  11.5 10.5 collective-permute-start
  14.6 7.3 collective-permute-start.1
  806.0 1.1 copy-start.2
  806.0 1.1 copy-start.3
  806.0 1.1 copy-start.4
  812.2 5.7 collective-permute-start.3
  814.1 4.7 collective-permute-start.2
  1595.9 1.0 copy-start.5
  1598.3 2.4 copy-start.1
Sparse Core Ops, SparseCore 0:
  11.5 743.6 all-gather.2
  811.5 736.3 all-gather.4
where the time goes:
time: 1610 us
  waiting for transfers between devices  1460 us (91%)
  local copies, waits for them, and re-layouts  92.8 us (6%)
  other arithmetic  24 us (1%)
  between operations  16.8 us (1%)
    all_gather x2, waiting for transfers between devices, extend(): lax.all_gather(strips, ('blk', 'ij'), axis=0, tiled=True)  1460 us
    broadcast_in_dim x6, local copies, waits for them, and re-layouts, pick_faces(): jnp.where(facing[:, :, None, None, None, None, None] == 1, piece[None, No...  77.9 us
  transfers between devices with their start and end apart: 6, of which 3 were waited for; matrix products, arithmetic and copies ran while one was open for 0% of the time, Pallas kernels for 0%

commit v1 on v0

--- a/solution.py
+++ b/solution.py
@@ -215,7 +215,14 @@
         )
         target = source * local_count + partner % local_count
         ghosts = pick_faces(
-            target, facing, lax.all_gather(strips, ("blk", "ij"), axis=0, tiled=True)
+            target,
+            facing,
+            jnp.concatenate(
+                lax.all_to_all(
+                    jnp.stack([strips] * lax.axis_size(("blk", "ij"))), ("blk", "ij"), 0, 0
+                ),
+                axis=0,
+            ),
         )
         ghosts = jnp.where(twisted[:, :, None, None, None, None] == 1, ghosts[..., ::-1], ghosts)
         ghosts = jnp.moveaxis(ghosts * factor, 2, -1)

time: 1610 us -> 489 us (0.30)
  the two profiles are of different devices: /device:TPU:99 before, /device:TPU:1 now
where the time goes in v1:
time: 489 us; the launch traced here: 479 us
  waiting for transfers between devices  200 us (41%)
  local copies, waits for them, and re-layouts  190 us (39%)
  other arithmetic  51.5 us (11%)
  starting transfers between devices  34.1 us (7%)
    all_to_all x2, waiting for transfers between devices, extend(): lax.all_to_all(jnp.stack([strips] * lax.axis_size(('blk', 'ij'))), ('blk'...  193 us
    unnamed x27, local copies, waits for them, and re-layouts  95.4 us
    broadcast_in_dim x6, local copies, waits for them, and re-layouts, pick_faces(): jnp.where(facing[:, :, None, None, None, None, None] == 1, piece[None, No...  65.4 us
    all_to_all x2, other arithmetic, extend(): lax.all_to_all(jnp.stack([strips] * lax.axis_size(('blk', 'ij'))), ('blk'...  31.3 us
    all_to_all x2, starting transfers between devices, extend(): lax.all_to_all(jnp.stack([strips] * lax.axis_size(('blk', 'ij'))), ('blk'...  24.3 us
    reshape x2, local copies, waits for them, and re-layouts, extend(): jnp.concatenate(lax.all_to_all(jnp.stack([strips] * lax.axis_size(('blk',...  16.9 us
  transfers between devices with their start and end apart: 6, of which 4 were waited for; matrix products, arithmetic and copies ran while one was open for 1% of the time, Pallas kernels for 0%

profile of v1, /device:TPU:1, one launch (start us, length us, event | category | flops | bytes accessed | tf_op | source)
XLA Modules:
  0.0 478.9 jit_solution(17619554864893886509)
XLA Ops:
  4.1 6.7 %broadcast_bitcast_fusion.1 = f32[256,1,2,5,7,2,32]{6,5,4,3,2,1,0:T(2,128)} fusion(f32[2,2,5,7,32]{4,1,3,2,0:T(2,128)S(1)} %maximum_bitcast_fusion), kind=kLoop, calls=%fused_computation.607 | loop fusion | bytes 4605440
  10.8 21.2 %reshape.2210 = f32[256,1,4480]{2,1,0:T(1,128)} reshape(f32[256,1,2,5,7,2,32]{6,5,4,3,2,1,0:T(2,128)} %broadcast_bitcast_fusion.1) | data formatting | bytes 9175040
  32.0 16.5 %all-to-all-start = ((f32[256,1,4480]{2,1,0:T(1,128)}), f32[256,1,4480]{2,1,0:T(1,128)}, u32[]{:S(2)}, u32[]{:S(2)}) async-start(f32[256,1,4480]{2,1,0:T(1,128)} %reshape.2210), calls=%async_computation | async-start | bytes 9175040 | tf_op jit(solution)/shard_map/all_to_all | solution.py:221
  48.7 3.3 collective-permute-start
  59.4 96.5 %all-to-all-done = f32[256,1,4480]{2,1,0:T(1,128)} async-done(((f32[256,1,4480]{2,1,0:T(1,128)}), f32[256,1,4480]{2,1,0:T(1,128)}, u32[]{:S(2)}, u32[]{:S(2)}) %all-to-all-start) | async-done | bytes 4587552 | tf_op jit(solution)/shard_map/all_to_all | solution.py:221
  156.4 15.6 %reduce.10 = f32[256,4480]{1,0:T(8,128)} reduce(f32[256,1,4480]{2,1,0:T(1,128)} %all-to-all-done, f32[]{:T(128)} %broadcast.1245), dimensions={1}, to_apply=%all_to_all.6.reduce_sub_computation | reduce | bytes 9175044 | tf_op jit(solution)/shard_map/all_to_all | solution.py:221
  172.0 19.0 %reshape.2211 = f32[256,1,2,5,7,2,32]{6,5,4,3,2,1,0:T(2,128)} reshape(f32[256,4480]{1,0:T(8,128)} %reduce.10) | data formatting | bytes 9175040
  191.0 8.4 %bitcast_bitcast_fusion.1 = f32[256,2,2,5,7,32]{5,2,4,3,1,0:T(2,128)S(1)} fusion(f32[256,1,2,5,7,2,32]{6,5,4,3,2,1,0:T(2,128)} %reshape.2211), kind=kLoop, calls=%fused_computation.605 | loop fusion | bytes 9175040 | tf_op jit(solution)/shard_map/reshape | solution.py:220
  199.4 10.2 %slice_bitcast_fusion.3 = (f32[256,2,5,7,32]{4,1,3,2,0:T(2,128)}, f32[256,2,5,7,32]{4,1,3,2,0:T(2,128)}) fusion(f32[256,2,2,5,7,32]{5,2,4,3,1,0:T(2,128)S(1)} %bitcast_bitcast_fusion.1), kind=kLoop, calls=%fused_computation.4 | loop fusion | bytes 9175040 | tf_op jit(solution)/shard_map/jit(_where)/broadcast_in_dim | solution.py:179
  209.6 11.1 %copy.244 = f32[256,2,5,7,32]{0,4,3,2,1:T(8,128)} copy(f32[256,2,5,7,32]{4,1,3,2,0:T(2,128)} %get-tuple-element.68) | data formatting | bytes 4587520 | tf_op jit(solution)/shard_map/jit(_where)/broadcast_in_dim | solution.py:179
  220.7 11.5 %copy.245 = f32[256,2,5,7,32]{0,4,3,2,1:T(8,128)} copy(f32[256,2,5,7,32]{4,1,3,2,0:T(2,128)} %get-tuple-element.69) | data formatting | bytes 4587520 | tf_op jit(solution)/shard_map/jit(_where)/broadcast_in_dim | solution.py:179
  232.3 3.1 select_reduce_fusion.1
  246.4 6.7 %broadcast_bitcast_fusion = f32[256,1,2,5,7,2,32]{6,5,4,3,2,1,0:T(2,128)} fusion(f32[2,2,5,7,32]{4,1,3,2,0:T(2,128)S(1)} %maximum_bitcast_fusion.1), kind=kLoop, calls=%fused_computation.606 | loop fusion | bytes 4605440
  253.1 21.2 %reshape.2212 = f32[256,1,4480]{2,1,0:T(1,128)} reshape(f32[256,1,2,5,7,2,32]{6,5,4,3,2,1,0:T(2,128)} %broadcast_bitcast_fusion) | data formatting | bytes 9175040
  274.3 7.7 %all-to-all-start.1 = ((f32[256,1,4480]{2,1,0:T(1,128)}), f32[256,1,4480]{2,1,0:T(1,128)}, u32[]{:S(2)}, u32[]{:S(2)}) async-start(f32[256,1,4480]{2,1,0:T(1,128)} %reshape.2212), calls=%async_computation.1 | async-start | bytes 9175040 | tf_op jit(solution)/shard_map/all_to_all | solution.py:221
  283.5 4.0 collective-permute-start.2
  287.6 5.1 %collective-permute-done.3 = f32[1,5,7,2,128]{4,3,2,1,0:T(2,128)S(1)} collective-permute-done((f32[1,5,7,2,128]{4,3,2,1,0:T(2,128)S(1)}, f32[1,5,7,2,128]{4,3,2,1,0:T(2,128)S(1)}, u32[]{:S(2)}, u32[]{:S(2)}) %collective-permute-start.3) | collective-permute-done | bytes 35872 | tf_op jit(solution)/shard_map/ppermute | solution.py:20
  292.9 96.6 %all-to-all-done.1 = f32[256,1,4480]{2,1,0:T(1,128)} async-done(((f32[256,1,4480]{2,1,0:T(1,128)}), f32[256,1,4480]{2,1,0:T(1,128)}, u32[]{:S(2)}, u32[]{:S(2)}) %all-to-all-start.1) | async-done | bytes 4587552 | tf_op jit(solution)/shard_map/all_to_all | solution.py:221
  389.5 15.6 %reduce.11 = f32[256,4480]{1,0:T(8,128)} reduce(f32[256,1,4480]{2,1,0:T(1,128)} %all-to-all-done.1, f32[]{:T(128)} %broadcast.1245), dimensions={1}, to_apply=%all_to_all.7.reduce_sub_computation | reduce | bytes 9175044 | tf_op jit(solution)/shard_map/all_to_all | solution.py:221
  405.2 19.0 %reshape.2213 = f32[256,1,2,5,7,2,32]{6,5,4,3,2,1,0:T(2,128)} reshape(f32[256,4480]{1,0:T(8,128)} %reduce.11) | data formatting | bytes 9175040
  424.1 8.4 %bitcast_bitcast_fusion = f32[256,2,2,5,7,32]{5,2,4,3,1,0:T(2,128)S(1)} fusion(f32[256,1,2,5,7,2,32]{6,5,4,3,2,1,0:T(2,128)} %reshape.2213), kind=kLoop, calls=%fused_computation.604 | loop fusion | bytes 9175040 | tf_op jit(solution)/shard_map/reshape | solution.py:220
  432.6 10.2 %slice_bitcast_fusion.1 = (f32[256,2,5,7,32]{4,1,3,2,0:T(2,128)}, f32[256,2,5,7,32]{4,1,3,2,0:T(2,128)}) fusion(f32[256,2,2,5,7,32]{5,2,4,3,1,0:T(2,128)S(1)} %bitcast_bitcast_fusion), kind=kLoop, calls=%fused_computation.2 | loop fusion | bytes 9175040 | tf_op jit(solution)/shard_map/jit(_where)/broadcast_in_dim | solution.py:179
  442.7 11.1 %copy.277 = f32[256,2,5,7,32]{0,4,3,2,1:T(8,128)} copy(f32[256,2,5,7,32]{4,1,3,2,0:T(2,128)} %get-tuple-element.66) | data formatting | bytes 4587520 | tf_op jit(solution)/shard_map/jit(_where)/broadcast_in_dim | solution.py:179
  453.9 11.3 %copy.278 = f32[256,2,5,7,32]{0,4,3,2,1:T(8,128)} copy(f32[256,2,5,7,32]{4,1,3,2,0:T(2,128)} %get-tuple-element.67) | data formatting | bytes 4587520 | tf_op jit(solution)/shard_map/jit(_where)/broadcast_in_dim | solution.py:179
  (188 shorter events, 35.0 us)
Async XLA Ops:
  32.0 123.9 %all-to-all-start = ((f32[256,1,4480]{2,1,0:T(1,128)}), f32[256,1,4480]{2,1,0:T(1,128)}, u32[]{:S(2)}, u32[]{:S(2)}) async-start(f32[256,1,4480]{2,1,0:T(1,128)} %reshape.2210), calls=%async_computation | async-start | bytes 9175040 | tf_op jit(solution)/shard_map/all_to_all | solution.py:221
  48.5 4.8 copy-start.6
  48.5 7.3 %copy-start.3 = (s32[32,2]{0,1:T(2,128)S(1)}, s32[32,2]{0,1:T(2,128)}, u32[]{:S(2)}) copy-start(s32[32,2]{0,1:T(2,128)} %param.16) | copy-start | bytes 772
  48.6 7.3 %copy-start.4 = (s32[32,2]{0,1:T(2,128)S(1)}, s32[32,2]{0,1:T(2,128)}, u32[]{:S(2)}) copy-start(s32[32,2]{0,1:T(2,128)} %param.15) | copy-start | bytes 772
  48.6 8.3 %copy-start.5 = (s32[32,2]{0,1:T(2,128)S(1)}, s32[32,2]{0,1:T(2,128)}, u32[]{:S(2)}) copy-start(s32[32,2]{0,1:T(2,128)} %param.17) | copy-start | bytes 772
  48.7 10.6 %collective-permute-start = (f32[1,5,7,2,128]{4,3,2,1,0:T(2,128)S(1)}, f32[1,5,7,2,128]{4,3,2,1,0:T(2,128)S(1)}, u32[]{:S(2)}, u32[]{:S(2)}) collective-permute-start(f32[1,5,7,2,128]{4,3,2,1,0:T(2,128)S(1)} %slice.1247), channel_id=1, source_target_pairs={{0,1},{1,2},{2,3},{3,4},{4,5},{5,6},{6,7},{8,9},{9,10},{10,11},{11... | collective-permute-start | bytes 107528 | tf_op jit(solution)/shard_map/ppermute | solution.py:19
  52.0 7.3 %collective-permute-start.1 = (f32[1,5,7,2,128]{4,3,2,1,0:T(2,128)S(1)}, f32[1,5,7,2,128]{4,3,2,1,0:T(2,128)S(1)}, u32[]{:S(2)}, u32[]{:S(2)}) collective-permute-start(f32[1,5,7,2,128]{4,3,2,1,0:T(2,128)S(1)} %fusion.282), channel_id=1, source_target_pairs={{1,0},{2,1},{3,2},{4,3},{5,4},{6,5},{7,6},{9,8},{10,9},{11,10},{12... | collective-permute-start | bytes 107528 | tf_op jit(solution)/shard_map/ppermute | solution.py:20
  242.8 1.0 copy-start
  242.9 1.0 copy-start.1
  242.9 1.0 copy-start.2
  274.3 115.2 %all-to-all-start.1 = ((f32[256,1,4480]{2,1,0:T(1,128)}), f32[256,1,4480]{2,1,0:T(1,128)}, u32[]{:S(2)}, u32[]{:S(2)}) async-start(f32[256,1,4480]{2,1,0:T(1,128)} %reshape.2212), calls=%async_computation.1 | async-start | bytes 9175040 | tf_op jit(solution)/shard_map/all_to_all | solution.py:221
  282.1 10.6 %collective-permute-start.3 = (f32[1,5,7,2,128]{4,3,2,1,0:T(2,128)S(1)}, f32[1,5,7,2,128]{4,3,2,1,0:T(2,128)S(1)}, u32[]{:S(2)}, u32[]{:S(2)}) collective-permute-start(f32[1,5,7,2,128]{4,3,2,1,0:T(2,128)S(1)} %get-tuple-element.110), channel_id=1, source_target_pairs={{1,0},{2,1},{3,2},{4,3},{5,4},{6,5},{7,6},{9,8},{10,9},{11,10},{12... | collective-permute-start | bytes 107528 | tf_op jit(solution)/shard_map/ppermute | solution.py:20
  283.5 9.3 %collective-permute-start.2 = (f32[1,5,7,2,128]{4,3,2,1,0:T(2,128)S(1)}, f32[1,5,7,2,128]{4,3,2,1,0:T(2,128)S(1)}, u32[]{:S(2)}, u32[]{:S(2)}) collective-permute-start(f32[1,5,7,2,128]{4,3,2,1,0:T(2,128)S(1)} %fusion.230), channel_id=1, source_target_pairs={{0,1},{1,2},{2,3},{3,4},{4,5},{5,6},{6,7},{8,9},{9,10},{10,11},{11... | collective-permute-start | bytes 107528 | tf_op jit(solution)/shard_map/ppermute | solution.py:19
